TPU v7x, 512 devices: a whole 4x4x16 slice. The times are simulated.
512 devices in a mesh: band: 8 (over x, core), blk: 64 (over y, z).
Axes of the slice: x: 4, y: 4, z: 16, core: 2. Of those that a mesh axis runs over, the one named last changes fastest.
Arguments:
- amps: bfloat16 [2560, 64, 128], P(None, 'blk'), may hold values from -6 to 6
- beam: float32 [8, 2560], P('band'), may hold values from 0.2 to 1
- legendre: bfloat16 [64, 2560, 256], P('blk'), as said below
- m_values: int32 [64], replicated, may hold values from 0 to 2559, as said below
- cycle_order: int32 [256], replicated, may hold values from 0 to 255, each once
- pixel_counts: int32 [256], replicated, may hold values from 512 to 4096, as said below
- inv_noise: float32 [8, 256, 4096], P('band', 'blk'), may hold values from 0.1 to 2
Outputs:
- amps_out: float32 [2560, 64, 128], P('band', 'blk')
Inputs may be any that keep to these rules, and one draw needn't show every extreme that they name: `m_values`: distinct orders; both 0 and 2559 occur. legendre[m, l, s] is zero wherever l < m_values[m]. `pixel_counts`: some cycle has exactly 4096 pixels.
All inputs are finite; a program needn't handle non-finite values.
Results may differ from a plain program's by a relative error of at most 0.0017.
Values may be sent and summed in bfloat16 or wider, within the bound.
A program may use at most 64 MiB of HBM per device.

v0:
```python
import math

import jax
import jax.numpy as jnp
from jax import lax
from jax.sharding import Mesh
from jax.sharding import PartitionSpec as P

PIX = 4096
BLK = ("blk_0", "blk_1")


def cut_along(array, dim, peers):
    before, after = (array.shape[:dim], array.shape[dim + 1 :])
    return jnp.moveaxis(array.reshape(*before, peers, -1, *after), dim, 0)


def in_order(pieces, dim):
    pieces = jnp.moveaxis(pieces, 0, dim)
    shape = pieces.shape
    return pieces.reshape(*shape[:dim], shape[dim] * shape[dim + 1], *shape[dim + 2 :])


def exchange_in_order(pieces, axes, order):
    inside = pieces.shape[1:]
    out = pieces.reshape(*(lax.axis_size(a) for a in axes), *inside)
    for k in order:
        out = lax.all_to_all(out, axes[k], k, k, tiled=True)
    return out.reshape(-1, *inside)


def one_axis_at_a_time(array, axes, order, split_dim, concat_dim):
    pieces = cut_along(array, split_dim, lax.axis_size(axes))
    return in_order(exchange_in_order(pieces, axes, order), concat_dim)


def sum_at_owner(array, axis, dim):
    peers = lax.axis_size(axis)
    pieces = lax.all_to_all(cut_along(array, dim, peers), axis, 0, 0, tiled=True)
    return jnp.sum(pieces, axis=0)


def cycle_table(order_ids, cycle_id, pixel_count, pixels):
    pixel_idx = jnp.arange(pixels, dtype=jnp.int32)
    product_mod = order_ids[:, None] * pixel_idx[None, :] % pixel_count
    parity = cycle_id % 2
    numerator = (2 * product_mod + order_ids[:, None] * parity) % (2 * pixel_count)
    phase_angle = numerator.astype(jnp.float32) * (
        jnp.float32(math.pi) / pixel_count.astype(jnp.float32)
    )
    inside = (pixel_idx < pixel_count)[None, :]
    norm_scale = lax.rsqrt(pixel_count.astype(jnp.float32))
    cos_part = jnp.where(inside, jnp.cos(phase_angle) * norm_scale, jnp.float32(0.0))
    sin_part = jnp.where(inside, -jnp.sin(phase_angle) * norm_scale, jnp.float32(0.0))
    return jnp.stack([cos_part, sin_part], axis=1).reshape(2 * order_ids.shape[0], pixels)


def cycle_pass(modes_in, phase_table, weights):
    orders = modes_in.shape[0]
    chains = modes_in.shape[1] // 2
    modes_flat = modes_in.reshape(2 * orders, chains)
    pixel_field = lax.dot_general(
        modes_flat, phase_table, (((0,), (0,)), ((), ())), precision=lax.Precision.HIGHEST
    )
    weighted_field = pixel_field * weights[None, :]
    projected = lax.dot_general(
        phase_table, weighted_field, (((1,), (1,)), ((), ())), precision=lax.Precision.HIGHEST
    )
    return projected.reshape(orders, 2 * chains)


def shards(amps, beam, legendre, m_values, cycle_order, pixel_counts, inv_noise):
    gains = beam[0]
    weighted = (amps.astype(jnp.float32) * gains[:, None, None]).astype(jnp.bfloat16)
    synth = jnp.einsum("mlr,lmc->rmc", legendre, weighted, preferred_element_type=jnp.float32)
    cycle_local = lax.all_to_all(synth, BLK, split_axis=0, concat_axis=1, tiled=True)
    cycles_here = inv_noise.shape[1]
    all_cycles = cycle_order.shape[0]
    cycle_ids = lax.dynamic_slice_in_dim(
        cycle_order, lax.axis_index(BLK) * cycles_here, cycles_here
    )
    matches = cycle_ids[:, None] == jnp.arange(all_cycles, dtype=jnp.int32)[None, :]
    local_counts = jnp.sum(jnp.where(matches, pixel_counts[None, :], 0), axis=1)

    def cycle_one(packed):
        phase_table = cycle_table(m_values, packed[1], packed[2], PIX)
        return cycle_pass(packed[0], phase_table, packed[3])

    projected = lax.map(cycle_one, (cycle_local, cycle_ids, local_counts, inv_noise[0]))
    proj_half = one_axis_at_a_time(projected.astype(jnp.bfloat16), BLK, (0, 1), 1, 0)
    partial_rows = jnp.einsum(
        "mlr,rmc->lmc", legendre, proj_half, preferred_element_type=jnp.float32
    )
    return sum_at_owner(partial_rows * gains[:, None, None], "band", 0)


def solution(mesh):
    finer = Mesh(mesh.devices.reshape(mesh.shape["band"], 4, 16), ("band", "blk_0", "blk_1"))
    placed = (
        P(None, BLK, None),
        P("band", None),
        P(BLK, None, None),
        P(),
        P(),
        P(),
        P("band", BLK, None),
    )
    return jax.shard_map(
        shards, mesh=finer, in_specs=placed, out_specs=P("band", BLK, None), check_vma=False
    )
```

profile of v0, /device:TPU:1, one launch (start us, length us, event | category | flops | bytes accessed | tf_op | source)
XLA Modules:
  0.0 259.6 jit_solution(5468367568842101152)
XLA Ops:
  1.3 1.9 fusion.14
  4.0 19.5 %all-to-all-start = ((f32[256,1,128]{2,1,0:T(1,128)}), f32[256,1,128]{2,1,0:T(1,128)}, u32[]{:S(2)}, u32[]{:S(2)}) async-start(f32[256,1,128]{2,1,0:T(1,128)} %copy.40), calls=%async_computation | async-start | bytes 262144 | tf_op jit(solution)/shard_map/all_to_all | solution.py:76
  23.9 13.8 %all-to-all-done = f32[256,1,128]{2,1,0:T(1,128)} async-done(((f32[256,1,128]{2,1,0:T(1,128)}), f32[256,1,128]{2,1,0:T(1,128)}, u32[]{:S(2)}, u32[]{:S(2)}) %all-to-all-start) | async-done | bytes 131104 | tf_op jit(solution)/shard_map/all_to_all | solution.py:76
  37.7 168.5 %while.12 = (s32[]{:T(128)}, bf16[4,64,128]{2,1,0:T(8,128)(2,1)}, s32[4]{0:T(128)S(1)}, s32[64]{0:T(128)S(1)}, s32[4]{0:T(128)S(1)}, /*index=5*/f32[4,64,128]{2,...) while((s32[]{:T(128)}, bf16[4,64,128]{2,1,0:T(8,128)(2,1)}, ...), condition=%wide.region_2.3_spmd, body=%wide.region_1.2_spmd.sunk | while | flops 812388480 | bytes 21276536 | solution.py:89
  44.2 24.2 %multiply_select_fusion.3 = (f32[64,1,4096]{2,0,1:T(8,128)S(1)}, f32[64,1,4096]{2,0,1:T(8,128)S(1)}) fusion(f32[]{:T(128)S(6)} %rsqrt.7, f32[]{:T(128)S(6)} %div.7, pred[]{:T(512)S(6)} %lt.114, s32[]{:T(128)S(6)} %select_n.136, s32[64]{0:T(128)S(1)} %broadcast_multiply_fusion.2, pred[]{:T(512)S(6)} %lt.116, s32[]{:T(128)S(6)} %select_n.138, ...), kind=kLoop, calls=%fused_computation.10.clone.1 | loop fusion | flops 6291456 | bytes 2101778 | tf_op jit(solution)/shard_map/while/body/eval_jaxpr/jit(_where)/select_n | solution.py:53
  68.6 3.0 %copy.50 = f32[64,2,4096]{2,1,0:T(2,128)} copy(f32[64,2,4096]{2,0,1:T(8,128)S(1)} %pad_maximum_fusion.2) | data formatting | bytes 4194304 | tf_op jit(solution)/shard_map/while/body/eval_jaxpr/stack | solution.py:55
  71.5 2.7 %reshape.258 = f32[128,4096]{1,0:T(8,128)S(1)} reshape(f32[64,2,4096]{2,1,0:T(2,128)} %copy.50) | data formatting | bytes 4194304 | tf_op jit(solution)/shard_map/while/body/eval_jaxpr/reshape | solution.py:55
  77.3 1.8 fusion.35
  86.3 24.2 %multiply_select_fusion.3 = (f32[64,1,4096]{2,0,1:T(8,128)S(1)}, f32[64,1,4096]{2,0,1:T(8,128)S(1)}) fusion(f32[]{:T(128)S(6)} %rsqrt.7, f32[]{:T(128)S(6)} %div.7, pred[]{:T(512)S(6)} %lt.114, s32[]{:T(128)S(6)} %select_n.136, s32[64]{0:T(128)S(1)} %broadcast_multiply_fusion.2, pred[]{:T(512)S(6)} %lt.116, s32[]{:T(128)S(6)} %select_n.138, ...), kind=kLoop, calls=%fused_computation.10.clone.1 | loop fusion | flops 6291456 | bytes 2101778 | tf_op jit(solution)/shard_map/while/body/eval_jaxpr/jit(_where)/select_n | solution.py:53
  110.7 3.0 %copy.50 = f32[64,2,4096]{2,1,0:T(2,128)} copy(f32[64,2,4096]{2,0,1:T(8,128)S(1)} %pad_maximum_fusion.2) | data formatting | bytes 4194304 | tf_op jit(solution)/shard_map/while/body/eval_jaxpr/stack | solution.py:55
  113.7 2.7 %reshape.258 = f32[128,4096]{1,0:T(8,128)S(1)} reshape(f32[64,2,4096]{2,1,0:T(2,128)} %copy.50) | data formatting | bytes 4194304 | tf_op jit(solution)/shard_map/while/body/eval_jaxpr/reshape | solution.py:55
  119.5 1.8 fusion.35
  128.4 24.2 %multiply_select_fusion.3 = (f32[64,1,4096]{2,0,1:T(8,128)S(1)}, f32[64,1,4096]{2,0,1:T(8,128)S(1)}) fusion(f32[]{:T(128)S(6)} %rsqrt.7, f32[]{:T(128)S(6)} %div.7, pred[]{:T(512)S(6)} %lt.114, s32[]{:T(128)S(6)} %select_n.136, s32[64]{0:T(128)S(1)} %broadcast_multiply_fusion.2, pred[]{:T(512)S(6)} %lt.116, s32[]{:T(128)S(6)} %select_n.138, ...), kind=kLoop, calls=%fused_computation.10.clone.1 | loop fusion | flops 6291456 | bytes 2101778 | tf_op jit(solution)/shard_map/while/body/eval_jaxpr/jit(_where)/select_n | solution.py:53
  152.8 3.0 %copy.50 = f32[64,2,4096]{2,1,0:T(2,128)} copy(f32[64,2,4096]{2,0,1:T(8,128)S(1)} %pad_maximum_fusion.2) | data formatting | bytes 4194304 | tf_op jit(solution)/shard_map/while/body/eval_jaxpr/stack | solution.py:55
  155.8 2.7 %reshape.258 = f32[128,4096]{1,0:T(8,128)S(1)} reshape(f32[64,2,4096]{2,1,0:T(2,128)} %copy.50) | data formatting | bytes 4194304 | tf_op jit(solution)/shard_map/while/body/eval_jaxpr/reshape | solution.py:55
  161.6 1.8 fusion.35
  170.6 24.2 %multiply_select_fusion.3 = (f32[64,1,4096]{2,0,1:T(8,128)S(1)}, f32[64,1,4096]{2,0,1:T(8,128)S(1)}) fusion(f32[]{:T(128)S(6)} %rsqrt.7, f32[]{:T(128)S(6)} %div.7, pred[]{:T(512)S(6)} %lt.114, s32[]{:T(128)S(6)} %select_n.136, s32[64]{0:T(128)S(1)} %broadcast_multiply_fusion.2, pred[]{:T(512)S(6)} %lt.116, s32[]{:T(128)S(6)} %select_n.138, ...), kind=kLoop, calls=%fused_computation.10.clone.1 | loop fusion | flops 6291456 | bytes 2101778 | tf_op jit(solution)/shard_map/while/body/eval_jaxpr/jit(_where)/select_n | solution.py:53
  195.0 3.0 %copy.50 = f32[64,2,4096]{2,1,0:T(2,128)} copy(f32[64,2,4096]{2,0,1:T(8,128)S(1)} %pad_maximum_fusion.2) | data formatting | bytes 4194304 | tf_op jit(solution)/shard_map/while/body/eval_jaxpr/stack | solution.py:55
  197.9 2.7 %reshape.258 = f32[128,4096]{1,0:T(8,128)S(1)} reshape(f32[64,2,4096]{2,1,0:T(2,128)} %copy.50) | data formatting | bytes 4194304 | tf_op jit(solution)/shard_map/while/body/eval_jaxpr/reshape | solution.py:55
  203.7 1.8 fusion.35
  207.1 8.1 %all_to_all.33 = bf16[4,16,4,1,128]{4,2,1,3,0:T(4,128)(2,1)S(1)} all-to-all(bf16[4,16,4,1,128]{4,2,1,3,0:T(4,128)(2,1)S(1)} %bitcast.67), channel_id=1, replica_groups=mesh['band'=8,'blk_0'=4,'blk_1'=16] {'blk_0'}, dimensions={0} | all-to-all | bytes 131072 | tf_op jit(solution)/shard_map/all_to_all | solution.py:28
  215.2 15.5 %all_to_all.34 = bf16[4,16,4,1,128]{4,2,0,3,1:T(4,128)(2,1)S(1)} all-to-all(bf16[4,16,4,1,128]{4,2,0,3,1:T(4,128)(2,1)S(1)} %copy.43), channel_id=1, replica_groups=mesh['band'=8,'blk_0'=4,'blk_1'=16] {'blk_1'}, dimensions={1} | all-to-all | bytes 131072 | tf_op jit(solution)/shard_map/all_to_all | solution.py:28
  231.4 1.5 copy.45
  232.8 26.0 %all_to_all.35 = f32[8,320,1,128]{3,1,2,0:T(8,128)S(1)} all-to-all(f32[8,320,1,128]{3,1,2,0:T(8,128)} %bitcast.64), channel_id=1, replica_groups=mesh['band'=8,'blk_0'=4,'blk_1'=16] {'band'}, dimensions={0} | all-to-all | bytes 2621440 | tf_op jit(solution)/shard_map/all_to_all | solution.py:39
  (62 shorter events, 27.8 us)
Async XLA Ops:
  0.0 1.3 copy-start
  1.3 22.3 %copy-start.3 = (s32[256]{0:T(256)S(1)}, s32[256]{0:T(256)}, u32[]{:S(2)}) copy-start(s32[256]{0:T(256)} %param.13) | copy-start | bytes 3076
  1.3 22.3 %copy-start.2 = (s32[256]{0:T(256)S(1)}, s32[256]{0:T(256)}, u32[]{:S(2)}) copy-start(s32[256]{0:T(256)} %param.14) | copy-start | bytes 3076
  1.3 36.4 %copy-start.1 = (s32[64]{0:T(128)S(1)}, s32[64]{0:T(128)}, u32[]{:S(2)}) copy-start(s32[64]{0:T(128)} %param.12) | copy-start | bytes 772
  4.0 33.7 %all-to-all-start = ((f32[256,1,128]{2,1,0:T(1,128)}), f32[256,1,128]{2,1,0:T(1,128)}, u32[]{:S(2)}, u32[]{:S(2)}) async-start(f32[256,1,128]{2,1,0:T(1,128)} %copy.40), calls=%async_computation | async-start | bytes 262144 | tf_op jit(solution)/shard_map/all_to_all | solution.py:76
where the time goes:
time: 261 us; the launch traced here: 260 us
  other arithmetic  102 us (39%)
  blocking collectives  49.6 us (19%)
  local copies, waits for them, and re-layouts  41.4 us (16%)
  starting transfers between devices  19.5 us (7%)
  loops' own time  18.8 us (7%)
  matrix products  14.5 us (6%)
  waiting for transfers between devices  13.8 us (5%)
    select_n x4, other arithmetic, cycle_table(): jnp.where(inside, jnp.cos(phase_angle) * norm_scale, jnp.float32(0.0))  96.8 us
    all_to_all x1, blocking collectives, sum_at_owner(): lax.all_to_all(cut_along(array, dim, peers), axis, 0, 0, tiled=True)  26 us
    all_to_all x2, blocking collectives, exchange_in_order(): out = lax.all_to_all(out, axes[k], k, k, tiled=True)  23.6 us
    all_to_all x1, starting transfers between devices, shards(): lax.all_to_all(synth, BLK, split_axis=0, concat_axis=1, tiled=True)  19.5 us
    another operation x1, loops' own time, shards(): lax.map(cycle_one, (cycle_local, cycle_ids, local_counts, inv_noise[0]))  18.8 us
    all_to_all x1, waiting for transfers between devices, shards(): lax.all_to_all(synth, BLK, split_axis=0, concat_axis=1, tiled=True)  13.8 us
    another operation x4, local copies, waits for them, and re-layouts, cycle_table(): jnp.stack([cos_part, sin_part], axis=1)  11.9 us
    dynamic_slice x16, local copies, waits for them, and re-layouts, shards(): lax.map(cycle_one, (cycle_local, cycle_ids, local_counts, inv_noise[0]))  11.9 us
  transfers between devices with their start and end apart: 1, of which 1 were waited for; matrix products, arithmetic and copies ran while one was open for 0% of the time, Pallas kernels for 0%

commit v1 on v0

v1 whole, which is shorter than its diff:
```python
import functools
import math

import jax
import jax.numpy as jnp
from jax import lax
from jax.experimental import pallas as pl
from jax.experimental.pallas import tpu as pltpu
from jax.sharding import PartitionSpec as P

MESH = pl.DeviceIdType.MESH
F32, BF16, I32 = jnp.float32, jnp.bfloat16, jnp.int32
LANES = 128
WIDE = 512
NY = 4


def dot_nt(a, b):
    return lax.dot_general(a, b, (((1,), (1,)), ((), ())), preferred_element_type=F32)


def split(x):
    high = x.astype(BF16)
    return high, (x - high.astype(F32)).astype(BF16)


def remainder(x, count, inverse):
    r = x - jnp.floor(x * inverse) * count
    r = jnp.where(r < 0.0, r + count, r)
    return jnp.where(r >= count, r - count, r)


def turn(doubled, count, inverse):
    k = jnp.floor(doubled * inverse + 0.5)
    phi = (doubled - k * count) * (inverse * jnp.float32(math.pi / 2))
    sq = phi * phi
    sin = phi + phi * sq * (-1.6666654611e-1 + sq * (8.3321608736e-3 + sq * -1.9515295891e-4))
    cos = 1.0 - 0.5 * sq + sq * sq * (
        4.166664568298827e-2 + sq * (-1.388731625493765e-3 + sq * 2.443315711809948e-5)
    )
    ki = k.astype(I32)
    odd = (ki & 1) == 1
    c = jnp.where(odd, sin, cos)
    s = jnp.where(odd, cos, sin)
    return jnp.where(((ki + 1) & 2) != 0, -c, c), jnp.where((ki & 2) != 0, s, -s)


def kernel(
    nband, nblk,
    m_ref, order_ref, counts_ref, amps_ref, beam_ref, leg_ref, noise_ref,
    out_ref,
    m_col, a_cos, a_sin, b_cos, b_sin, gram, flat, syn, got, stage, half, back, around, legp, beams, gains, inside,
    send_sem, recv_sem, own_sem, beam_sem, ag_send, ag_recv, fw_send, fw_recv,
):
    band = lax.axis_index("band")
    me = lax.axis_index("blk")
    nz = nblk // NY
    nx = nband // 2
    degrees = leg_ref.shape[0]
    cycles = leg_ref.shape[1]
    orders = m_col.shape[0]
    here = cycles // nblk
    pixels = noise_ref.shape[1]
    steps = pixels // WIDE
    chains = amps_ref.shape[1] // 2
    rows = degrees // nband
    my_y, my_z = me // nz, me % nz
    my_x, core = band // 2, band % 2

    def other_blk(t):
        u, v = t // NY, t % NY
        dz = nz // 2 + jnp.where(u % 2 == 0, u // 2, -((u + 1) // 2))
        return (my_y + v + 1) % NY * nz + (my_z + dz + nz) % nz

    def band_of(dx, dc):
        return (my_x + dx + nx) % nx * 2 + (core + dc) % 2

    others = [(dx, dc) for dx in range(nx) for dc in range(2) if (dx, dc) != (0, 0)]

    barrier = pltpu.get_barrier_semaphore()

    @pl.loop(0, nblk - 1)
    def _(t):
        pl.semaphore_signal(barrier, inc=1, device_id=(band, other_blk(t)), device_id_type=MESH)

    for dx, dc in others:
        pl.semaphore_signal(barrier, inc=1, device_id=(band_of(dx, dc), me), device_id_type=MESH)

    def synth_step(i, total):
        parts = []
        for h in range(2):
            at = pl.multiple_of(i * 2 * LANES + h * LANES, LANES)
            piece = amps_ref[pl.ds(at, LANES), :].astype(F32).T
            parts.append((piece * beam_ref[:, pl.ds(at, LANES)]).astype(BF16))
        weighted = jnp.concatenate(parts, axis=1)
        at = pl.multiple_of(i * 2 * LANES, LANES)
        return total + jnp.dot(weighted, leg_ref[pl.ds(at, 2 * LANES), :], preferred_element_type=F32)

    total = lax.fori_loop(0, degrees // (2 * LANES), synth_step, jnp.zeros((2 * chains, cycles), F32))
    flat[...] = total.T
    for i in range(here):
        syn[:, i, :] = flat[pl.ds(i, nblk, stride=here), :]

    @pl.loop(0, orders)
    def _(i):
        m_col[pl.ds(i, 1), :] = jnp.full((1, LANES), m_ref[i], I32).astype(F32)

    lane = lax.broadcasted_iota(I32, (1, LANES), 1)

    def cycle(i):
        q = order_ref[me * here + i]
        return counts_ref[q], q & 1

    m = m_col[...]
    count_v = jnp.full((1, LANES), 1, I32)
    parity_v = jnp.zeros((1, LANES), I32)
    pixel = lax.broadcasted_iota(I32, (1, pixels), 1)
    for i in range(here):
        n, parity = cycle(i)
        inside[i] = jnp.where(pixel < n, noise_ref[i : i + 1, :], 0.0)
        mine = lane // steps == i
        count_v = jnp.where(mine, n, count_v)
        parity_v = jnp.where(mine, parity, parity_v)
    count_v = count_v.astype(F32)
    inverse_v = 1.0 / count_v
    r = remainder(m * ((lane % steps) * WIDE).astype(F32), count_v, inverse_v)
    ca, sa = turn(4.0 * r + 2.0 * m * parity_v.astype(F32), count_v, inverse_v)
    for t in range(here * steps):
        a_cos[t] = jnp.broadcast_to(ca[:, t : t + 1], (orders, LANES))
        a_sin[t] = jnp.broadcast_to(sa[:, t : t + 1], (orders, LANES))

    def form_gram(i):
        n, _ = cycle(i)
        count = jnp.full((1, LANES), n, I32).astype(F32)
        inverse = 1.0 / count
        for g in range(WIDE // LANES):
            r = remainder(m_col[...] * (lane + g * LANES).astype(F32), count, inverse)
            c, s = turn(4.0 * r, count, inverse)
            b_cos[:, g * LANES : (g + 1) * LANES] = c
            b_sin[:, g * LANES : (g + 1) * LANES] = s

        def step(a, acc):
            c1, s1 = a_cos[i * steps + a], a_sin[i * steps + a]
            left, right = [], []
            for g in range(WIDE // LANES):
                c2, s2 = b_cos[:, g * LANES : (g + 1) * LANES], b_sin[:, g * LANES : (g + 1) * LANES]
                at = pl.multiple_of(a * WIDE + g * LANES, LANES)
                w = inside[i, :, pl.ds(at, LANES)]
                c = c1 * c2 - s1 * s2
                s = s1 * c2 + c1 * s2
                ch, cl = split(c)
                sh, sl = split(s)
                left.append(jnp.concatenate([ch, sh, cl, sl], axis=0))
                ch, cl = split(c * w)
                sh, sl = split(s * w)
                right.append(jnp.concatenate([ch, sh, cl, sl], axis=0))
            return acc + dot_nt(jnp.concatenate(left, axis=1), jnp.concatenate(right, axis=1))

        acc = lax.fori_loop(0, steps, step, jnp.zeros((4 * orders, 4 * orders), F32))
        two = 2 * orders
        full = (acc[:two, :two] + acc[:two, two:]) + (acc[two:, :two] + acc[two:, two:])
        full = full * inverse[:, :two] if two <= LANES else full * inverse[:, :1]
        full = jnp.concatenate([full[:orders], pltpu.roll(full[orders:], orders, 1)], axis=0)
        gram[i] = jnp.concatenate(split(full), axis=0)

    @pl.loop(0, here // 2)
    def _(i):
        form_gram(i)

    pl.semaphore_wait(barrier, nblk - 1 + nband - 1)

    @pl.loop(0, nblk - 1)
    def _(t):
        d = other_blk(t)
        pltpu.make_async_remote_copy(
            src_ref=syn.at[d], dst_ref=got.at[me], send_sem=send_sem.at[0], recv_sem=recv_sem.at[0],
            device_id=(band, d), device_id_type=MESH,
        ).start()

    pltpu.make_async_copy(syn.at[me], got.at[me], own_sem.at[0]).start()
    for dx, dc in others:
        pltpu.make_async_remote_copy(
            src_ref=beam_ref, dst_ref=beams.at[band], send_sem=beam_sem.at[0], recv_sem=beam_sem.at[1],
            device_id=(band_of(dx, dc), me), device_id_type=MESH,
        ).start()
    pltpu.make_async_copy(beam_ref, beams.at[band], own_sem.at[1]).start()

    @pl.loop(here // 2, here)
    def _(i):
        form_gram(i)

    row = lax.broadcasted_iota(I32, (cycles, cycles), 0)
    col = lax.broadcasted_iota(I32, (cycles, cycles), 1)
    pick = jnp.where(row == here * (col % nblk) + col // nblk, 1.0, 0.0).astype(BF16)
    mine = leg_ref[pl.ds(pl.multiple_of(band * rows, rows & -rows), rows), :]
    legp[...] = jnp.dot(mine, pick, preferred_element_type=F32).astype(BF16)

    pltpu.make_async_copy(syn.at[me], got.at[me], own_sem.at[0]).wait()
    most = got.at[pl.ds(0, nblk - 1)]
    pltpu.make_async_copy(most, most, recv_sem.at[0]).wait()

    for i in range(here):
        x = got[:, i, :]
        xh, xl = split(jnp.concatenate([x, pltpu.roll(x, chains, 1)], axis=0))
        y = jnp.dot(gram[i], jnp.concatenate([xh, xl], axis=1), preferred_element_type=F32)
        wide, two = 2 * chains, 2 * orders
        y = (y[:two, :wide] + y[:two, wide:]) + (y[two:, :wide] + y[two:, wide:])
        lane_k = lax.broadcasted_iota(I32, (orders, wide), 1)
        stage[:, i, :] = jnp.where(lane_k < chains, y[:orders], y[orders:])
    half[...] = stage[...].astype(BF16)

    @pl.loop(0, nblk - 1)
    def _(t):
        d = other_blk(t)
        pltpu.make_async_remote_copy(
            src_ref=half.at[d], dst_ref=back.at[me], send_sem=send_sem.at[1], recv_sem=recv_sem.at[1],
            device_id=(band, d), device_id_type=MESH,
        ).start()

    pltpu.make_async_copy(half.at[me], back.at[me], own_sem.at[2]).start()

    pltpu.make_async_copy(beam_ref, beams.at[band], own_sem.at[1]).wait()
    pltpu.make_async_copy(beams.at[pl.ds(0, nband - 1)], beams.at[pl.ds(0, nband - 1)], beam_sem.at[1]).wait()
    first = band * rows
    base = first // LANES * LANES
    span = -(-(rows + LANES // 2) // LANES) * LANES
    for b in range(nband):
        line = beams[b, :, pl.ds(pl.multiple_of(base, LANES), span)]
        if rows % LANES:
            line = jnp.where(first - base > 0, pltpu.roll(line, span - LANES // 2, 1), line)
        for g in range(-(-rows // LANES)):
            size = min(LANES, rows - g * LANES)
            block = jnp.broadcast_to(line[:, g * LANES : (g + 1) * LANES], (LANES, LANES)).T
            gains[b, g * LANES : g * LANES + size, :] = block[:size]

    pltpu.make_async_copy(half.at[me], back.at[me], own_sem.at[2]).wait()
    most = back.at[pl.ds(0, nblk - 1)]
    pltpu.make_async_copy(most, most, recv_sem.at[1]).wait()
    got[...] = back[...].astype(F32)
    for i in range(here):
        around[band, i * nblk : (i + 1) * nblk, :] = got[:, i, :].astype(BF16)

    for dx in range(1, nx):
        pltpu.make_async_remote_copy(
            src_ref=around.at[band], dst_ref=around.at[band], send_sem=ag_send.at[dx], recv_sem=ag_recv.at[dx],
            device_id=(band_of(dx, 0), me), device_id_type=MESH,
        ).start()

    def hand_on(dx):
        slot = band_of(-dx, 0)
        return pltpu.make_async_remote_copy(
            src_ref=around.at[slot], dst_ref=around.at[slot], send_sem=fw_send.at[dx], recv_sem=fw_recv.at[dx],
            device_id=(band_of(0, 1), me), device_id_type=MESH,
        )

    def from_chip(dx):
        slot = band_of(-dx, 0)
        return pltpu.make_async_remote_copy(
            src_ref=around.at[slot], dst_ref=around.at[slot], send_sem=ag_send.at[dx], recv_sem=ag_recv.at[dx],
            device_id=(band_of(dx, 0), me), device_id_type=MESH,
        )

    def term(slot):
        return gains[slot] * jnp.dot(legp[...], around[slot], preferred_element_type=F32)

    hand_on(0).start()
    out_ref[...] = term(band)
    arrivals = [1, nx - 1] + list(range(2, nx - 1)) if nx > 2 else list(range(1, nx))
    for dx in arrivals:
        from_chip(dx).wait_recv()
        hand_on(dx).start()
        out_ref[...] += term(band_of(-dx, 0))
    for dx in [0] + arrivals:
        slot = band_of(-dx, 1)
        pltpu.make_async_copy(around.at[slot], around.at[slot], fw_recv.at[dx]).wait()
        out_ref[...] += term(slot)

    for dx in range(1, nx):
        from_chip(dx).wait_send()
    for dx in range(nx):
        hand_on(dx).wait_send()
    for k in range(nband - 1):
        pltpu.make_async_copy(beam_ref, beam_ref, beam_sem.at[0]).wait()
    most = syn.at[pl.ds(0, nblk - 1)]
    pltpu.make_async_copy(most, most, send_sem.at[0]).wait()
    most = half.at[pl.ds(0, nblk - 1)]
    pltpu.make_async_copy(most, most, send_sem.at[1]).wait()


def shards(nband, nblk, amps, beam, legendre, m_values, cycle_order, pixel_counts, inv_noise):
    degrees, _, wide = amps.shape
    cycles = legendre.shape[2]
    orders = m_values.shape[0]
    here = cycles // nblk
    pixels = inv_noise.shape[2]
    rows = degrees // nband
    steps = pixels // WIDE
    vmem = pl.BlockSpec(memory_space=pltpu.VMEM)
    smem = pl.BlockSpec(memory_space=pltpu.SMEM)
    dma = pltpu.SemaphoreType.DMA
    out = pl.pallas_call(
        functools.partial(kernel, nband, nblk),
        out_shape=jax.ShapeDtypeStruct((rows, wide), F32),
        in_specs=[smem, smem, smem, vmem, vmem, vmem, vmem],
        out_specs=vmem,
        scratch_shapes=[
            pltpu.VMEM((orders, LANES), F32),
            pltpu.VMEM((here * steps, orders, LANES), F32),
            pltpu.VMEM((here * steps, orders, LANES), F32),
            pltpu.VMEM((orders, WIDE), F32),
            pltpu.VMEM((orders, WIDE), F32),
            pltpu.VMEM((here, 4 * orders, 2 * orders), BF16),
            pltpu.VMEM((cycles, wide), F32),
            pltpu.VMEM((nblk, here, wide), F32),
            pltpu.VMEM((nblk, here, wide), F32),
            pltpu.VMEM((orders, here, wide), F32),
            pltpu.VMEM((orders, here, wide), BF16),
            pltpu.VMEM((nblk, here, wide), BF16),
            pltpu.VMEM((nband, cycles, wide), BF16),
            pltpu.VMEM((rows, cycles), BF16),
            pltpu.VMEM((nband, 1, degrees), F32),
            pltpu.VMEM((nband, rows, wide), F32),
            pltpu.VMEM((here, 1, pixels), F32),
            dma((2,)),
            dma((2,)),
            dma((3,)),
            dma((2,)),
            dma((nband // 2,)),
            dma((nband // 2,)),
            dma((nband // 2,)),
            dma((nband // 2,)),
        ],
        compiler_params=pltpu.CompilerParams(
            collective_id=0, has_side_effects=True, vmem_limit_bytes=60 * 1024 * 1024
        ),
    )(
        m_values, cycle_order, pixel_counts,
        amps.reshape(degrees, wide), beam, legendre.reshape(degrees, cycles), inv_noise.reshape(here, pixels),
    )
    return out.reshape(rows, 1, wide)


def solution(mesh):
    nband, nblk = mesh.shape["band"], mesh.shape["blk"]
    placed = (
        P(None, "blk", None),
        P("band", None),
        P("blk", None, None),
        P(),
        P(),
        P(),
        P("band", "blk", None),
    )
    return jax.shard_map(
        functools.partial(shards, nband, nblk),
        mesh=mesh, in_specs=placed, out_specs=P("band", "blk", None), check_vma=False,
    )
```

time: 261 us -> 52.3 us (0.20)
  other arithmetic: 102 us -> 0 us
  Pallas kernels: 0 us -> 50.5 us
  blocking collectives: 49.6 us -> 0 us
  local copies, waits for them, and re-layouts: 41.4 us -> 1.59 us
  starting transfers between devices: 19.5 us -> 0 us
  loops' own time: 18.8 us -> 0 us
  matrix products: 14.5 us -> 0 us
  waiting for transfers between devices: 13.8 us -> 0 us
    select_n x4 -> x0, other arithmetic: 96.8 us -> none  [cycle_table(): jnp.where(inside, jnp.cos(phase_angle) * norm_scale, jnp.float32(0.0))]
    pallas_call x0 -> x1, Pallas kernels: none -> 50.5 us  [shards(): pl.pallas_call(functools.partial(kernel, nband, nblk), out_shape=jax.Shap...]
    all_to_all x3 -> x0, blocking collectives: 49.6 us -> none  [the longest x1 26 us: sum_at_owner(): lax.all_to_all(cut_along(array, dim, peers), axis, 0, 0, tiled=True)]
    all_to_all x1 -> x0, starting transfers between devices: 19.5 us -> none  [shards(): lax.all_to_all(synth, BLK, split_axis=0, concat_axis=1, tiled=True)]
    another operation x1 -> x0, loops' own time: 18.8 us -> none  [shards(): lax.map(cycle_one, (cycle_local, cycle_ids, local_counts, inv_noise[0]))]
    dot_general x10 -> x0, matrix products: 14.5 us -> none  [the longest x4 7.14 us: cycle_pass(): lax.dot_general(phase_table, weighted_field, (((1,), (1,)), ((), ())), pr...]
    all_to_all x1 -> x0, waiting for transfers between devices: 13.8 us -> none  [shards(): lax.all_to_all(synth, BLK, split_axis=0, concat_axis=1, tiled=True)]
    dynamic_slice x17 -> x0, local copies, waits for them, and re-layouts: 12 us -> none  [the longest x16 11.9 us: shards(): lax.map(cycle_one, (cycle_local, cycle_ids, local_counts, inv_noise[0]))]
  transfers between devices with their start and end apart: 1 -> 0, of which waited for: 1 -> 0; matrix products, arithmetic and copies ran while one was open for 0% -> 0% of each run, Pallas kernels for 0% -> 0%
where the time goes in v1:
time: 52.3 us; the launch traced here: 52.1 us
  Pallas kernels  50.5 us (97%)
  local copies, waits for them, and re-layouts  1.59 us (3%)
    pallas_call x1, Pallas kernels, shards(): pl.pallas_call(functools.partial(kernel, nband, nblk), out_shape=jax.Shap...  50.5 us
    unnamed x1, local copies, waits for them, and re-layouts  1.59 us

profile of v1, /device:TPU:1, one launch (start us, length us, event | category | flops | bytes accessed | tf_op | source)
XLA Modules:
  0.0 52.1 jit_solution(4021408214883206690)
XLA Ops:
  0.0 50.5 %shard_map.73 = f32[320,128]{1,0:T(8,128)} custom-call(s32[64]{0:T(128)} %m_ref.1, s32[256]{0:T(256)} %order_ref.1, s32[256]{0:T(256)} %counts_ref.1, bf16[2560,128]{1,0:T(8,128)(2,1)} %bitcast.8, f32[1,2560]{1,0:T(1,128)} %beam_ref.1, bf16[2560,256]{1,0:T(8,128)(2,1)} %bitcast.6, f32[4,4096]{1,0:T(4,128)} %bitcast.9), custom_call_target="tpu_custom_call" | custom-call | tf_op jit(solution)/shard_map/pallas_call | solution.py:301
  50.5 1.6 %copy.10 = f32[320,1,128]{2,1,0:T(1,128)} copy(f32[320,1,128]{2,1,0:T(1,128)} %bitcast.7) | data formatting | bytes 327680

commit v2 on v1

--- a/solution.py
+++ b/solution.py
@@ -64,24 +64,29 @@
     steps = pixels // WIDE
     chains = amps_ref.shape[1] // 2
     rows = degrees // nband
-    my_y, my_z = me // nz, me % nz
-    my_x, core = band // 2, band % 2
-
-    def other_blk(t):
-        u, v = t // NY, t % NY
-        dz = nz // 2 + jnp.where(u % 2 == 0, u // 2, -((u + 1) // 2))
-        return (my_y + v + 1) % NY * nz + (my_z + dz + nz) % nz
+    my_y, my_z = me // nz, me & (nz - 1)
+    my_x, core = band // 2, band & 1
+
+    column = [((my_y + k) & (NY - 1)) * nz for k in range(NY)]
+
+    def each_other(act):
+        @pl.loop(0, nz - 1)
+        def _(u):
+            z = (my_z + nz // 2 + ((u >> 1) ^ -(u & 1))) & (nz - 1)
+            for k in (2, 1, 3, 0):
+                act(column[k] + z)
+
+        for k in (2, 1, 3):
+            act(column[k] + my_z)
 
     def band_of(dx, dc):
-        return (my_x + dx + nx) % nx * 2 + (core + dc) % 2
+        return ((my_x + dx) & (nx - 1)) * 2 + ((core + dc) & 1)
 
     others = [(dx, dc) for dx in range(nx) for dc in range(2) if (dx, dc) != (0, 0)]
 
     barrier = pltpu.get_barrier_semaphore()
 
-    @pl.loop(0, nblk - 1)
-    def _(t):
-        pl.semaphore_signal(barrier, inc=1, device_id=(band, other_blk(t)), device_id_type=MESH)
+    each_other(lambda d: pl.semaphore_signal(barrier, inc=1, device_id=(band, d), device_id_type=MESH))
 
     for dx, dc in others:
         pl.semaphore_signal(barrier, inc=1, device_id=(band_of(dx, dc), me), device_id_type=MESH)
@@ -117,7 +122,7 @@
     pixel = lax.broadcasted_iota(I32, (1, pixels), 1)
     for i in range(here):
         n, parity = cycle(i)
-        inside[i] = jnp.where(pixel < n, noise_ref[i : i + 1, :], 0.0)
+        inside[i] = jnp.where(pixel < n, jnp.sqrt(noise_ref[i : i + 1, :]), 0.0)
         mine = lane // steps == i
         count_v = jnp.where(mine, n, count_v)
         parity_v = jnp.where(mine, parity, parity_v)
@@ -141,41 +146,37 @@
 
         def step(a, acc):
             c1, s1 = a_cos[i * steps + a], a_sin[i * steps + a]
-            left, right = [], []
+            highs, lows = [], []
             for g in range(WIDE // LANES):
                 c2, s2 = b_cos[:, g * LANES : (g + 1) * LANES], b_sin[:, g * LANES : (g + 1) * LANES]
-                at = pl.multiple_of(a * WIDE + g * LANES, LANES)
-                w = inside[i, :, pl.ds(at, LANES)]
-                c = c1 * c2 - s1 * s2
-                s = s1 * c2 + c1 * s2
-                ch, cl = split(c)
-                sh, sl = split(s)
-                left.append(jnp.concatenate([ch, sh, cl, sl], axis=0))
-                ch, cl = split(c * w)
-                sh, sl = split(s * w)
-                right.append(jnp.concatenate([ch, sh, cl, sl], axis=0))
-            return acc + dot_nt(jnp.concatenate(left, axis=1), jnp.concatenate(right, axis=1))
-
-        acc = lax.fori_loop(0, steps, step, jnp.zeros((4 * orders, 4 * orders), F32))
+                w = inside[i, :, pl.ds(pl.multiple_of(a * WIDE + g * LANES, LANES), LANES)]
+                ch, cl = split((c1 * c2 - s1 * s2) * w)
+                sh, sl = split((s1 * c2 + c1 * s2) * w)
+                highs.append(jnp.concatenate([ch, sh], axis=0))
+                lows.append(jnp.concatenate([cl, sl], axis=0))
+            high, low = jnp.concatenate(highs, axis=1), jnp.concatenate(lows, axis=1)
+            return acc + dot_nt(high, jnp.concatenate([high, low], axis=0))
+
         two = 2 * orders
-        full = (acc[:two, :two] + acc[:two, two:]) + (acc[two:, :two] + acc[two:, two:])
+        acc = lax.fori_loop(0, steps, step, jnp.zeros((two, 2 * two), F32))
+        cross = acc[:, two:]
+        full = acc[:, :two] + (cross + cross.T)
         full = full * inverse[:, :two] if two <= LANES else full * inverse[:, :1]
         full = jnp.concatenate([full[:orders], pltpu.roll(full[orders:], orders, 1)], axis=0)
         gram[i] = jnp.concatenate(split(full), axis=0)
 
-    @pl.loop(0, here // 2)
-    def _(i):
-        form_gram(i)
-
     pl.semaphore_wait(barrier, nblk - 1 + nband - 1)
 
-    @pl.loop(0, nblk - 1)
-    def _(t):
-        d = other_blk(t)
-        pltpu.make_async_remote_copy(
-            src_ref=syn.at[d], dst_ref=got.at[me], send_sem=send_sem.at[0], recv_sem=recv_sem.at[0],
-            device_id=(band, d), device_id_type=MESH,
-        ).start()
+    def send_to(source, target, k):
+        def act(d):
+            pltpu.make_async_remote_copy(
+                src_ref=source.at[d], dst_ref=target.at[me], send_sem=send_sem.at[k], recv_sem=recv_sem.at[k],
+                device_id=(band, d), device_id_type=MESH,
+            ).start()
+
+        each_other(act)
+
+    send_to(syn, got, 0)
 
     pltpu.make_async_copy(syn.at[me], got.at[me], own_sem.at[0]).start()
     for dx, dc in others:
@@ -185,7 +186,7 @@
         ).start()
     pltpu.make_async_copy(beam_ref, beams.at[band], own_sem.at[1]).start()
 
-    @pl.loop(here // 2, here)
+    @pl.loop(0, here)
     def _(i):
         form_gram(i)
 
@@ -209,13 +210,7 @@
         stage[:, i, :] = jnp.where(lane_k < chains, y[:orders], y[orders:])
     half[...] = stage[...].astype(BF16)
 
-    @pl.loop(0, nblk - 1)
-    def _(t):
-        d = other_blk(t)
-        pltpu.make_async_remote_copy(
-            src_ref=half.at[d], dst_ref=back.at[me], send_sem=send_sem.at[1], recv_sem=recv_sem.at[1],
-            device_id=(band, d), device_id_type=MESH,
-        ).start()
+    send_to(half, back, 1)
 
     pltpu.make_async_copy(half.at[me], back.at[me], own_sem.at[2]).start()
 

time: 52.3 us -> 47.7 us (0.912)
  Pallas kernels: 50.5 us -> 45.9 us
    pallas_call x1, Pallas kernels: 50.5 us -> 45.9 us  [shards(): pl.pallas_call(functools.partial(kernel, nband, nblk), out_shape=jax.Shap...]
where the time goes in v2:
time: 47.7 us; the launch traced here: 47.5 us
  Pallas kernels  45.9 us (96%)
  local copies, waits for them, and re-layouts  1.59 us (3%)
    pallas_call x1, Pallas kernels, shards(): pl.pallas_call(functools.partial(kernel, nband, nblk), out_shape=jax.Shap...  45.9 us
    unnamed x1, local copies, waits for them, and re-layouts  1.59 us

profile of v2, /device:TPU:1, one launch (start us, length us, event | category | flops | bytes accessed | tf_op | source)
XLA Modules:
  0.0 47.5 jit_solution(2723147646252049259)
XLA Ops:
  0.0 45.9 %shard_map.73 = f32[320,128]{1,0:T(8,128)} custom-call(s32[64]{0:T(128)} %m_ref.1, s32[256]{0:T(256)} %order_ref.1, s32[256]{0:T(256)} %counts_ref.1, bf16[2560,128]{1,0:T(8,128)(2,1)} %bitcast.8, f32[1,2560]{1,0:T(1,128)} %beam_ref.1, bf16[2560,256]{1,0:T(8,128)(2,1)} %bitcast.6, f32[4,4096]{1,0:T(4,128)} %bitcast.9), custom_call_target="tpu_custom_call" | custom-call | tf_op jit(solution)/shard_map/pallas_call | solution.py:296
  45.9 1.6 %copy.10 = f32[320,1,128]{2,1,0:T(1,128)} copy(f32[320,1,128]{2,1,0:T(1,128)} %bitcast.7) | data formatting | bytes 327680

commit v3 on v2

--- a/solution.py
+++ b/solution.py
@@ -13,6 +13,7 @@
 LANES = 128
 WIDE = 512
 NY = 4
+EARLY = 1
 
 
 def dot_nt(a, b):
@@ -47,8 +48,9 @@
 
 def kernel(
     nband, nblk,
-    m_ref, order_ref, counts_ref, amps_ref, beam_ref, leg_ref, noise_ref,
-    out_ref,
+    m_ref, order_ref, counts_ref, beam_ref, amps_in, leg_in, noise_in,
+    out_ref, rest_ref,
+    amps_ref, leg_ref, noise_ref, in_sem,
     m_col, a_cos, a_sin, b_cos, b_sin, gram, flat, syn, got, stage, half, back, around, legp, beams, gains, inside,
     send_sem, recv_sem, own_sem, beam_sem, ag_send, ag_recv, fw_send, fw_recv,
 ):
@@ -69,15 +71,18 @@
 
     column = [((my_y + k) & (NY - 1)) * nz for k in range(NY)]
 
-    def each_other(act):
-        @pl.loop(0, nz - 1)
+    turns = (2, 1, 3, 0)
+
+    def each_other(act, first, last):
+        @pl.loop(first, min(last, nz - 1))
         def _(u):
             z = (my_z + nz // 2 + ((u >> 1) ^ -(u & 1))) & (nz - 1)
-            for k in (2, 1, 3, 0):
-                act(column[k] + z)
-
-        for k in (2, 1, 3):
-            act(column[k] + my_z)
+            for j, k in enumerate(turns):
+                act(column[k] + z, u * NY + j)
+
+        if last == nz:
+            for j, k in enumerate(turns[:-1]):
+                act(column[k] + my_z, (nz - 1) * NY + j)
 
     def band_of(dx, dc):
         return ((my_x + dx) & (nx - 1)) * 2 + ((core + dc) & 1)
@@ -86,10 +91,20 @@
 
     barrier = pltpu.get_barrier_semaphore()
 
-    each_other(lambda d: pl.semaphore_signal(barrier, inc=1, device_id=(band, d), device_id_type=MESH))
+    loads = [
+        pltpu.make_async_copy(source, target, in_sem.at[k])
+        for k, (source, target) in enumerate(((amps_in, amps_ref), (leg_in, leg_ref), (noise_in, noise_ref)))
+    ]
+    for load in loads:
+        load.start()
+
+    each_other(lambda d, t: pl.semaphore_signal(barrier, inc=1, device_id=(band, d), device_id_type=MESH), 0, nz)
 
     for dx, dc in others:
         pl.semaphore_signal(barrier, inc=1, device_id=(band_of(dx, dc), me), device_id_type=MESH)
+
+    for load in loads:
+        load.wait()
 
     def synth_step(i, total):
         parts = []
@@ -106,7 +121,7 @@
     for i in range(here):
         syn[:, i, :] = flat[pl.ds(i, nblk, stride=here), :]
 
-    @pl.loop(0, orders)
+    @pl.loop(0, orders, unroll=8)
     def _(i):
         m_col[pl.ds(i, 1), :] = jnp.full((1, LANES), m_ref[i], I32).astype(F32)
 
@@ -123,29 +138,38 @@
     for i in range(here):
         n, parity = cycle(i)
         inside[i] = jnp.where(pixel < n, jnp.sqrt(noise_ref[i : i + 1, :]), 0.0)
-        mine = lane // steps == i
+        mine = lane // 16 == i
         count_v = jnp.where(mine, n, count_v)
         parity_v = jnp.where(mine, parity, parity_v)
     count_v = count_v.astype(F32)
     inverse_v = 1.0 / count_v
-    r = remainder(m * ((lane % steps) * WIDE).astype(F32), count_v, inverse_v)
+    entry = lane % 16
+    coarse = entry < steps
+    stride = jnp.where(coarse, entry * WIDE, (entry - steps) * LANES)
+    parity_v = jnp.where(coarse, parity_v, 0)
+    r = remainder(m * stride.astype(F32), count_v, inverse_v)
     ca, sa = turn(4.0 * r + 2.0 * m * parity_v.astype(F32), count_v, inverse_v)
-    for t in range(here * steps):
-        a_cos[t] = jnp.broadcast_to(ca[:, t : t + 1], (orders, LANES))
-        a_sin[t] = jnp.broadcast_to(sa[:, t : t + 1], (orders, LANES))
+    kinds = steps + WIDE // LANES
+    for i in range(here):
+        for e in range(kinds):
+            t = i * 16 + e
+            a_cos[i * kinds + e] = jnp.broadcast_to(ca[:, t : t + 1], (orders, LANES))
+            a_sin[i * kinds + e] = jnp.broadcast_to(sa[:, t : t + 1], (orders, LANES))
 
     def form_gram(i):
         n, _ = cycle(i)
         count = jnp.full((1, LANES), n, I32).astype(F32)
         inverse = 1.0 / count
-        for g in range(WIDE // LANES):
-            r = remainder(m_col[...] * (lane + g * LANES).astype(F32), count, inverse)
-            c, s = turn(4.0 * r, count, inverse)
-            b_cos[:, g * LANES : (g + 1) * LANES] = c
-            b_sin[:, g * LANES : (g + 1) * LANES] = s
+        r = remainder(m_col[...] * lane.astype(F32), count, inverse)
+        c2, s2 = turn(4.0 * r, count, inverse)
+        b_cos[:, :LANES], b_sin[:, :LANES] = c2, s2
+        for g in range(1, WIDE // LANES):
+            c1, s1 = a_cos[i * kinds + steps + g], a_sin[i * kinds + steps + g]
+            b_cos[:, g * LANES : (g + 1) * LANES] = c1 * c2 - s1 * s2
+            b_sin[:, g * LANES : (g + 1) * LANES] = s1 * c2 + c1 * s2
 
         def step(a, acc):
-            c1, s1 = a_cos[i * steps + a], a_sin[i * steps + a]
+            c1, s1 = a_cos[i * kinds + a], a_sin[i * kinds + a]
             highs, lows = [], []
             for g in range(WIDE // LANES):
                 c2, s2 = b_cos[:, g * LANES : (g + 1) * LANES], b_sin[:, g * LANES : (g + 1) * LANES]
@@ -165,19 +189,19 @@
         full = jnp.concatenate([full[:orders], pltpu.roll(full[orders:], orders, 1)], axis=0)
         gram[i] = jnp.concatenate(split(full), axis=0)
 
+    @pl.loop(0, EARLY)
+    def _(i):
+        form_gram(i)
+
     pl.semaphore_wait(barrier, nblk - 1 + nband - 1)
 
-    def send_to(source, target, k):
-        def act(d):
-            pltpu.make_async_remote_copy(
-                src_ref=source.at[d], dst_ref=target.at[me], send_sem=send_sem.at[k], recv_sem=recv_sem.at[k],
-                device_id=(band, d), device_id_type=MESH,
-            ).start()
-
-        each_other(act)
-
-    send_to(syn, got, 0)
-
+    def send(d, t):
+        pltpu.make_async_remote_copy(
+            src_ref=syn.at[d], dst_ref=got.at[me], send_sem=send_sem.at[0], recv_sem=recv_sem.at[0],
+            device_id=(band, d), device_id_type=MESH,
+        ).start()
+
+    each_other(send, 0, nz)
     pltpu.make_async_copy(syn.at[me], got.at[me], own_sem.at[0]).start()
     for dx, dc in others:
         pltpu.make_async_remote_copy(
@@ -186,13 +210,18 @@
         ).start()
     pltpu.make_async_copy(beam_ref, beams.at[band], own_sem.at[1]).start()
 
-    @pl.loop(0, here)
+    @pl.loop(EARLY, here)
     def _(i):
         form_gram(i)
 
     row = lax.broadcasted_iota(I32, (cycles, cycles), 0)
     col = lax.broadcasted_iota(I32, (cycles, cycles), 1)
-    pick = jnp.where(row == here * (col % nblk) + col // nblk, 1.0, 0.0).astype(BF16)
+    slot = col % (nblk // 2) + col // (cycles // 2) * (nblk // 2)
+    u, j = slot // NY, slot % NY
+    k = jnp.where(j == 3, 0, jnp.where(j == 2, 3, 2 - j))
+    z = (my_z - nz // 2 - ((u >> 1) ^ -(u & 1))) & (nz - 1)
+    source = ((my_y - k) & (NY - 1)) * nz + z
+    pick = jnp.where(row == here * source + col // (nblk // 2) % here, 1.0, 0.0).astype(BF16)
     mine = leg_ref[pl.ds(pl.multiple_of(band * rows, rows & -rows), rows), :]
     legp[...] = jnp.dot(mine, pick, preferred_element_type=F32).astype(BF16)
 
@@ -210,9 +239,17 @@
         stage[:, i, :] = jnp.where(lane_k < chains, y[:orders], y[orders:])
     half[...] = stage[...].astype(BF16)
 
-    send_to(half, back, 1)
-
-    pltpu.make_async_copy(half.at[me], back.at[me], own_sem.at[2]).start()
+    for g in range(2):
+
+        def send(d, t, g=g):
+            pltpu.make_async_remote_copy(
+                src_ref=half.at[d], dst_ref=back.at[t], send_sem=send_sem.at[1], recv_sem=recv_sem.at[1 + g],
+                device_id=(band, d), device_id_type=MESH,
+            ).start()
+
+        each_other(send, g * nz // 2, (g + 1) * nz // 2)
+
+    pltpu.make_async_copy(half.at[me], back.at[nblk - 1], own_sem.at[2]).start()
 
     pltpu.make_async_copy(beam_ref, beams.at[band], own_sem.at[1]).wait()
     pltpu.make_async_copy(beams.at[pl.ds(0, nband - 1)], beams.at[pl.ds(0, nband - 1)], beam_sem.at[1]).wait()
@@ -228,52 +265,67 @@
             block = jnp.broadcast_to(line[:, g * LANES : (g + 1) * LANES], (LANES, LANES)).T
             gains[b, g * LANES : g * LANES + size, :] = block[:size]
 
-    pltpu.make_async_copy(half.at[me], back.at[me], own_sem.at[2]).wait()
-    most = back.at[pl.ds(0, nblk - 1)]
-    pltpu.make_async_copy(most, most, recv_sem.at[1]).wait()
-    got[...] = back[...].astype(F32)
-    for i in range(here):
-        around[band, i * nblk : (i + 1) * nblk, :] = got[:, i, :].astype(BF16)
-
-    for dx in range(1, nx):
-        pltpu.make_async_remote_copy(
-            src_ref=around.at[band], dst_ref=around.at[band], send_sem=ag_send.at[dx], recv_sem=ag_recv.at[dx],
+    per = cycles // 2
+
+    def across(dx, g):
+        part = around.at[band, pl.ds(g * per, per)]
+        return pltpu.make_async_remote_copy(
+            src_ref=part, dst_ref=part, send_sem=ag_send.at[g * nx + dx], recv_sem=ag_recv.at[g * nx + dx],
             device_id=(band_of(dx, 0), me), device_id_type=MESH,
-        ).start()
-
-    def hand_on(dx):
-        slot = band_of(-dx, 0)
+        )
+
+    def arrival(sem, dx, dc, g):
+        part = around.at[band_of(-dx, dc), pl.ds(g * per, per)]
+        return pltpu.make_async_copy(part, part, sem.at[g * nx + dx])
+
+    def hand_on(dx, g):
+        part = around.at[band_of(-dx, 0), pl.ds(g * per, per)]
         return pltpu.make_async_remote_copy(
-            src_ref=around.at[slot], dst_ref=around.at[slot], send_sem=fw_send.at[dx], recv_sem=fw_recv.at[dx],
+            src_ref=part, dst_ref=part, send_sem=fw_send.at[g * nx + dx], recv_sem=fw_recv.at[g * nx + dx],
             device_id=(band_of(0, 1), me), device_id_type=MESH,
         )
 
-    def from_chip(dx):
-        slot = band_of(-dx, 0)
-        return pltpu.make_async_remote_copy(
-            src_ref=around.at[slot], dst_ref=around.at[slot], send_sem=ag_send.at[dx], recv_sem=ag_recv.at[dx],
-            device_id=(band_of(dx, 0), me), device_id_type=MESH,
-        )
-
-    def term(slot):
-        return gains[slot] * jnp.dot(legp[...], around[slot], preferred_element_type=F32)
-
-    hand_on(0).start()
-    out_ref[...] = term(band)
-    arrivals = [1, nx - 1] + list(range(2, nx - 1)) if nx > 2 else list(range(1, nx))
-    for dx in arrivals:
-        from_chip(dx).wait_recv()
-        hand_on(dx).start()
-        out_ref[...] += term(band_of(-dx, 0))
-    for dx in [0] + arrivals:
-        slot = band_of(-dx, 1)
-        pltpu.make_async_copy(around.at[slot], around.at[slot], fw_recv.at[dx]).wait()
-        out_ref[...] += term(slot)
-
-    for dx in range(1, nx):
-        from_chip(dx).wait_send()
-    for dx in range(nx):
-        hand_on(dx).wait_send()
+    hops = [nx // 2] + [dx for dx in range(1, nx) if dx != nx // 2]
+    for g in (1, 0):
+        lot = nblk // 2
+        if g == 1:
+            pltpu.make_async_copy(half.at[me], back.at[nblk - 1], own_sem.at[2]).wait()
+        most = back.at[pl.ds(g * lot, lot - g)]
+        pltpu.make_async_copy(most, most, recv_sem.at[1 + g]).wait()
+        stage[g * lot : (g + 1) * lot] = back[g * lot : (g + 1) * lot].astype(F32)
+        for i in range(here):
+            at = g * per + i * lot
+            around[band, at : at + lot, :] = stage[g * lot : (g + 1) * lot, i, :].astype(BF16)
+        for dx in hops:
+            across(dx, g).start()
+        hand_on(0, g).start()
+
+    ready = hops[1:] + hops[:1]
+    for g in (1, 0):
+        for dx in ready:
+            arrival(ag_recv, dx, 0, g).wait()
+            hand_on(dx, g).start()
+
+    def terms(slots):
+        total = None
+        for slot in slots:
+            one = gains[slot] * jnp.dot(legp[...], around[slot], preferred_element_type=F32)
+            total = one if total is None else total + one
+        return total
+
+    for g in (1, 0):
+        arrival(fw_recv, 0, 1, g).wait()
+    out_ref[...] = terms([band_of(-dx, 0) for dx in range(nx)] + [band_of(0, 1)])
+    for g in (1, 0):
+        for dx in ready:
+            arrival(fw_recv, dx, 1, g).wait()
+    rest_ref[...] = terms([band_of(-dx, 1) for dx in ready])
+
+    for g in (1, 0):
+        for dx in hops:
+            across(dx, g).wait_send()
+        for dx in range(nx):
+            hand_on(dx, g).wait_send()
     for k in range(nband - 1):
         pltpu.make_async_copy(beam_ref, beam_ref, beam_sem.at[0]).wait()
     most = syn.at[pl.ds(0, nblk - 1)]
@@ -291,17 +343,22 @@
     rows = degrees // nband
     steps = pixels // WIDE
     vmem = pl.BlockSpec(memory_space=pltpu.VMEM)
+    left = pl.BlockSpec(memory_space=pl.ANY)
     smem = pl.BlockSpec(memory_space=pltpu.SMEM)
     dma = pltpu.SemaphoreType.DMA
-    out = pl.pallas_call(
+    most, rest = pl.pallas_call(
         functools.partial(kernel, nband, nblk),
-        out_shape=jax.ShapeDtypeStruct((rows, wide), F32),
-        in_specs=[smem, smem, smem, vmem, vmem, vmem, vmem],
-        out_specs=vmem,
+        out_shape=[jax.ShapeDtypeStruct((rows, wide), F32)] * 2,
+        in_specs=[smem, smem, smem, vmem, left, left, left],
+        out_specs=[vmem, vmem],
         scratch_shapes=[
+            pltpu.VMEM((degrees, wide), BF16),
+            pltpu.VMEM((degrees, cycles), BF16),
+            pltpu.VMEM((here, pixels), F32),
+            dma((3,)),
             pltpu.VMEM((orders, LANES), F32),
-            pltpu.VMEM((here * steps, orders, LANES), F32),
-            pltpu.VMEM((here * steps, orders, LANES), F32),
+            pltpu.VMEM((here * (steps + WIDE // LANES), orders, LANES), F32),
+            pltpu.VMEM((here * (steps + WIDE // LANES), orders, LANES), F32),
             pltpu.VMEM((orders, WIDE), F32),
             pltpu.VMEM((orders, WIDE), F32),
             pltpu.VMEM((here, 4 * orders, 2 * orders), BF16),
@@ -317,22 +374,22 @@
             pltpu.VMEM((nband, rows, wide), F32),
             pltpu.VMEM((here, 1, pixels), F32),
             dma((2,)),
-            dma((2,)),
+            dma((3,)),
             dma((3,)),
             dma((2,)),
-            dma((nband // 2,)),
-            dma((nband // 2,)),
-            dma((nband // 2,)),
-            dma((nband // 2,)),
+            dma((nband,)),
+            dma((nband,)),
+            dma((nband,)),
+            dma((nband,)),
         ],
         compiler_params=pltpu.CompilerParams(
             collective_id=0, has_side_effects=True, vmem_limit_bytes=60 * 1024 * 1024
         ),
     )(
         m_values, cycle_order, pixel_counts,
-        amps.reshape(degrees, wide), beam, legendre.reshape(degrees, cycles), inv_noise.reshape(here, pixels),
+        beam, amps.reshape(degrees, wide), legendre.reshape(degrees, cycles), inv_noise.reshape(here, pixels),
     )
-    return out.reshape(rows, 1, wide)
+    return (most + rest).reshape(rows, 1, wide)
 
 
 def solution(mesh):

time: 47.7 us -> 46.8 us (0.981)
  other arithmetic: 0 us -> 1.68 us
  local copies, waits for them, and re-layouts: 1.59 us -> 0 us
  Pallas kernels: 45.9 us -> 44.9 us
    add x0 -> x1, other arithmetic: none -> 1.68 us  [shards(): return (most + rest).reshape(rows, 1, wide)]
    unnamed x1 -> x0, local copies, waits for them, and re-layouts: 1.59 us -> none
    pallas_call x1, Pallas kernels: 45.9 us -> 44.9 us  [shards(): pl.pallas_call(functools.partial(kernel, nband, nblk), out_shape=[jax.Sha...]
where the time goes in v3:
time: 46.8 us; the launch traced here: 46.6 us
  Pallas kernels  44.9 us (96%)
  other arithmetic  1.68 us (4%)
    pallas_call x1, Pallas kernels, shards(): pl.pallas_call(functools.partial(kernel, nband, nblk), out_shape=[jax.Sha...  44.9 us
    add x1, other arithmetic, shards(): return (most + rest).reshape(rows, 1, wide)  1.68 us

profile of v3, /device:TPU:1, one launch (start us, length us, event | category | flops | bytes accessed | tf_op | source)
XLA Modules:
  0.0 46.6 jit_solution(6998297234872031620)
XLA Ops:
  0.0 44.9 %shard_map.73 = (f32[320,128]{1,0:T(8,128)}, f32[320,128]{1,0:T(8,128)}) custom-call(s32[64]{0:T(128)} %m_ref.1, s32[256]{0:T(256)} %order_ref.1, s32[256]{0:T(256)} %counts_ref.1, f32[1,2560]{1,0:T(1,128)} %beam_ref.1, bf16[2560,128]{1,0:T(8,128)(2,1)} %bitcast.7, bf16[2560,256]{1,0:T(8,128)(2,1)} %bitcast.6, f32[4,4096]{1,0:T(4,128)} %bitcast.8), custom_call_target="tpu_custom_call" | custom-call | tf_op jit(solution)/shard_map/pallas_call | solution.py:349
  44.9 1.7 %add.3 = f32[320,128]{1,0:T(8,128)} add(f32[320,128]{1,0:T(8,128)} %get-tuple-element.7, f32[320,128]{1,0:T(8,128)} %get-tuple-element.8) | non-fusion elementwise | flops 40960 | bytes 491520 | tf_op jit(solution)/shard_map/add | solution.py:392

commit v4 on v3

--- a/solution.py
+++ b/solution.py
@@ -52,7 +52,7 @@
     out_ref, rest_ref,
     amps_ref, leg_ref, noise_ref, in_sem,
     m_col, a_cos, a_sin, b_cos, b_sin, gram, flat, syn, got, stage, half, back, around, legp, beams, gains, inside,
-    send_sem, recv_sem, own_sem, beam_sem, ag_send, ag_recv, fw_send, fw_recv,
+    send_sem, recv_sem, own_sem, beam_sem, ag_send, ag_recv,
 ):
     band = lax.axis_index("band")
     me = lax.axis_index("blk")
@@ -267,25 +267,21 @@
 
     per = cycles // 2
 
-    def across(dx, g):
+    def across(dx, dc, g):
         part = around.at[band, pl.ds(g * per, per)]
+        k = (g * nx + dx) * 2 + dc
         return pltpu.make_async_remote_copy(
-            src_ref=part, dst_ref=part, send_sem=ag_send.at[g * nx + dx], recv_sem=ag_recv.at[g * nx + dx],
-            device_id=(band_of(dx, 0), me), device_id_type=MESH,
+            src_ref=part, dst_ref=part, send_sem=ag_send.at[k], recv_sem=ag_recv.at[k],
+            device_id=(band_of(dx, dc), me), device_id_type=MESH,
         )
 
-    def arrival(sem, dx, dc, g):
+    def arrived(dx, dc, g):
         part = around.at[band_of(-dx, dc), pl.ds(g * per, per)]
-        return pltpu.make_async_copy(part, part, sem.at[g * nx + dx])
-
-    def hand_on(dx, g):
-        part = around.at[band_of(-dx, 0), pl.ds(g * per, per)]
-        return pltpu.make_async_remote_copy(
-            src_ref=part, dst_ref=part, send_sem=fw_send.at[g * nx + dx], recv_sem=fw_recv.at[g * nx + dx],
-            device_id=(band_of(0, 1), me), device_id_type=MESH,
-        )
-
-    hops = [nx // 2] + [dx for dx in range(1, nx) if dx != nx // 2]
+        pltpu.make_async_copy(part, part, ag_recv.at[(g * nx + dx) * 2 + dc]).wait()
+
+    far = nx // 2
+    near = [dx for dx in range(1, nx) if dx != far]
+    direct = [(far, 0), (far, 1), (0, 1)] + [(dx, dc) for dc in range(2) for dx in near]
     for g in (1, 0):
         lot = nblk // 2
         if g == 1:
@@ -296,36 +292,36 @@
         for i in range(here):
             at = g * per + i * lot
             around[band, at : at + lot, :] = stage[g * lot : (g + 1) * lot, i, :].astype(BF16)
-        for dx in hops:
-            across(dx, g).start()
-        hand_on(0, g).start()
-
-    ready = hops[1:] + hops[:1]
-    for g in (1, 0):
-        for dx in ready:
-            arrival(ag_recv, dx, 0, g).wait()
-            hand_on(dx, g).start()
+        for dx, dc in direct:
+            across(dx, dc, g).start()
 
     def terms(slots):
         total = None
-        for slot in slots:
-            one = gains[slot] * jnp.dot(legp[...], around[slot], preferred_element_type=F32)
-            total = one if total is None else total + one
+        for i in range(0, len(slots), 2):
+            pair = slots[i : i + 2]
+            side = jnp.concatenate([around[slot] for slot in pair], axis=1) if len(pair) == 2 else around[pair[0]]
+            both = jnp.dot(legp[...], side, preferred_element_type=F32)
+            wide = 2 * chains
+            for j, slot in enumerate(pair):
+                one = gains[slot] * both[:, j * wide : (j + 1) * wide]
+                total = one if total is None else total + one
         return total
 
     for g in (1, 0):
-        arrival(fw_recv, 0, 1, g).wait()
-    out_ref[...] = terms([band_of(-dx, 0) for dx in range(nx)] + [band_of(0, 1)])
+        arrived(0, 1, g)
+        arrived(far, 0, g)
+        for dx in near:
+            arrived(dx, 0, g)
+    out_ref[...] = terms([band, band_of(0, 1), band_of(-far, 0)] + [band_of(-dx, 0) for dx in near[:1]])
     for g in (1, 0):
-        for dx in ready:
-            arrival(fw_recv, dx, 1, g).wait()
-    rest_ref[...] = terms([band_of(-dx, 1) for dx in ready])
+        for dx in near:
+            arrived(dx, 1, g)
+        arrived(far, 1, g)
+    rest_ref[...] = terms([band_of(-dx, 0) for dx in near[1:]] + [band_of(-dx, 1) for dx in near] + [band_of(-far, 1)])
 
     for g in (1, 0):
-        for dx in hops:
-            across(dx, g).wait_send()
-        for dx in range(nx):
-            hand_on(dx, g).wait_send()
+        for dx, dc in direct:
+            across(dx, dc, g).wait_send()
     for k in range(nband - 1):
         pltpu.make_async_copy(beam_ref, beam_ref, beam_sem.at[0]).wait()
     most = syn.at[pl.ds(0, nblk - 1)]
@@ -348,7 +344,7 @@
     dma = pltpu.SemaphoreType.DMA
     most, rest = pl.pallas_call(
         functools.partial(kernel, nband, nblk),
-        out_shape=[jax.ShapeDtypeStruct((rows, wide), F32)] * 2,
+        out_shape=[pltpu.VMEM((rows, wide), F32)] * 2,
         in_specs=[smem, smem, smem, vmem, left, left, left],
         out_specs=[vmem, vmem],
         scratch_shapes=[
@@ -377,10 +373,8 @@
             dma((3,)),
             dma((3,)),
             dma((2,)),
-            dma((nband,)),
-            dma((nband,)),
-            dma((nband,)),
-            dma((nband,)),
+            dma((2 * nband,)),
+            dma((2 * nband,)),
         ],
         compiler_params=pltpu.CompilerParams(
             collective_id=0, has_side_effects=True, vmem_limit_bytes=60 * 1024 * 1024

time: 46.8 us -> 44.3 us (0.947)
  Pallas kernels: 44.9 us -> 43.4 us
  other arithmetic: 1.68 us -> 0.69 us
    pallas_call x1, Pallas kernels: 44.9 us -> 43.4 us  [shards(): pl.pallas_call(functools.partial(kernel, nband, nblk), out_shape=[pltpu.V...]
    add x1, other arithmetic: 1.68 us -> 0.69 us  [shards(): return (most + rest).reshape(rows, 1, wide)]
where the time goes in v4:
time: 44.3 us; the launch traced here: 44.1 us
  Pallas kernels  43.4 us (98%)
  other arithmetic  0.69 us (2%)
    pallas_call x1, Pallas kernels, shards(): pl.pallas_call(functools.partial(kernel, nband, nblk), out_shape=[pltpu.V...  43.4 us

profile of v4, /device:TPU:1, one launch (start us, length us, event | category | flops | bytes accessed | tf_op | source)
XLA Modules:
  0.0 44.1 jit_solution(4327092201912585639)
XLA Ops:
  0.0 43.4 %shard_map.73 = (f32[320,128]{1,0:T(8,128)S(1)}, f32[320,128]{1,0:T(8,128)S(1)}) custom-call(s32[64]{0:T(128)} %m_ref.1, s32[256]{0:T(256)} %order_ref.1, s32[256]{0:T(256)} %counts_ref.1, f32[1,2560]{1,0:T(1,128)} %beam_ref.1, bf16[2560,128]{1,0:T(8,128)(2,1)} %bitcast.7, bf16[2560,256]{1,0:T(8,128)(2,1)} %bitcast.6, f32[4,4096]{1,0:T(4,128)} %bitcast.8), custom_call_target="tpu_custom_call" | custom-call | tf_op jit(solution)/shard_map/pallas_call | solution.py:345
  43.4 0.7 %add.3 = f32[320,128]{1,0:T(8,128)} add(f32[320,128]{1,0:T(8,128)S(1)} %get-tuple-element.7, f32[320,128]{1,0:T(8,128)S(1)} %get-tuple-element.8) | non-fusion elementwise | flops 40960 | bytes 491520 | tf_op jit(solution)/shard_map/add | solution.py:386

commit v5 on v4

--- a/solution.py
+++ b/solution.py
@@ -48,9 +48,9 @@
 
 def kernel(
     nband, nblk,
-    m_ref, order_ref, counts_ref, beam_ref, amps_in, leg_in, noise_in,
+    m_in, order_in, counts_in, beam_in, amps_in, leg_in, noise_in,
     out_ref, rest_ref,
-    amps_ref, leg_ref, noise_ref, in_sem,
+    m_ref, order_ref, counts_ref, beam_ref, amps_ref, leg_ref, noise_ref, in_sem,
     m_col, a_cos, a_sin, b_cos, b_sin, gram, flat, syn, got, stage, half, back, around, legp, beams, gains, inside,
     send_sem, recv_sem, own_sem, beam_sem, ag_send, ag_recv,
 ):
@@ -93,15 +93,20 @@
 
     loads = [
         pltpu.make_async_copy(source, target, in_sem.at[k])
-        for k, (source, target) in enumerate(((amps_in, amps_ref), (leg_in, leg_ref), (noise_in, noise_ref)))
+        for k, (source, target) in enumerate(
+            (
+                (amps_in, amps_ref), (beam_in, beam_ref), (leg_in, leg_ref), (m_in, m_ref),
+                (order_in, order_ref), (counts_in, counts_ref), (noise_in, noise_ref),
+            )
+        )
     ]
+    each_other(lambda d, t: pl.semaphore_signal(barrier, inc=1, device_id=(band, d), device_id_type=MESH), 0, nz)
+
+    for dx, dc in others:
+        pl.semaphore_signal(barrier, inc=1, device_id=(band_of(dx, dc), me), device_id_type=MESH)
+
     for load in loads:
         load.start()
-
-    each_other(lambda d, t: pl.semaphore_signal(barrier, inc=1, device_id=(band, d), device_id_type=MESH), 0, nz)
-
-    for dx, dc in others:
-        pl.semaphore_signal(barrier, inc=1, device_id=(band_of(dx, dc), me), device_id_type=MESH)
 
     for load in loads:
         load.wait()
@@ -340,18 +345,21 @@
     steps = pixels // WIDE
     vmem = pl.BlockSpec(memory_space=pltpu.VMEM)
     left = pl.BlockSpec(memory_space=pl.ANY)
-    smem = pl.BlockSpec(memory_space=pltpu.SMEM)
     dma = pltpu.SemaphoreType.DMA
     most, rest = pl.pallas_call(
         functools.partial(kernel, nband, nblk),
         out_shape=[pltpu.VMEM((rows, wide), F32)] * 2,
-        in_specs=[smem, smem, smem, vmem, left, left, left],
+        in_specs=[left] * 7,
         out_specs=[vmem, vmem],
         scratch_shapes=[
+            pltpu.SMEM((orders,), I32),
+            pltpu.SMEM((cycles,), I32),
+            pltpu.SMEM((cycles,), I32),
+            pltpu.VMEM((1, degrees), F32),
             pltpu.VMEM((degrees, wide), BF16),
             pltpu.VMEM((degrees, cycles), BF16),
             pltpu.VMEM((here, pixels), F32),
-            dma((3,)),
+            dma((7,)),
             pltpu.VMEM((orders, LANES), F32),
             pltpu.VMEM((here * (steps + WIDE // LANES), orders, LANES), F32),
             pltpu.VMEM((here * (steps + WIDE // LANES), orders, LANES), F32),

time: 44.3 us -> 43.9 us (level)
  no operation moved by 1% of the time
where the time goes in v5:
time: 43.9 us; the launch traced here: 43.7 us
  Pallas kernels  43 us (98%)
  other arithmetic  0.69 us (2%)
    pallas_call x1, Pallas kernels, shards(): pl.pallas_call(functools.partial(kernel, nband, nblk), out_shape=[pltpu.V...  43 us

profile of v5, /device:TPU:1, one launch (start us, length us, event | category | flops | bytes accessed | tf_op | source)
XLA Modules:
  0.0 43.7 jit_solution(13672076662778245443)
XLA Ops:
  0.0 43.0 %shard_map.73 = (f32[320,128]{1,0:T(8,128)S(1)}, f32[320,128]{1,0:T(8,128)S(1)}) custom-call(s32[64]{0:T(128)} %m_in.1, s32[256]{0:T(256)} %order_in.1, s32[256]{0:T(256)} %counts_in.1, f32[1,2560]{1,0:T(1,128)} %beam_in.1, bf16[2560,128]{1,0:T(8,128)(2,1)} %bitcast.7, bf16[2560,256]{1,0:T(8,128)(2,1)} %bitcast.6, f32[4,4096]{1,0:T(4,128)} %bitcast.8), custom_call_target="tpu_custom_call" | custom-call | tf_op jit(solution)/shard_map/pallas_call | solution.py:349
  43.0 0.7 %add.3 = f32[320,128]{1,0:T(8,128)} add(f32[320,128]{1,0:T(8,128)S(1)} %get-tuple-element.7, f32[320,128]{1,0:T(8,128)S(1)} %get-tuple-element.8) | non-fusion elementwise | flops 40960 | bytes 491520 | tf_op jit(solution)/shard_map/add | solution.py:394

commit v6 on v5

--- a/solution.py
+++ b/solution.py
@@ -13,7 +13,7 @@
 LANES = 128
 WIDE = 512
 NY = 4
-EARLY = 1
+EARLY = 0
 
 
 def dot_nt(a, b):
@@ -219,6 +219,32 @@
     def _(i):
         form_gram(i)
 
+    pltpu.make_async_copy(syn.at[me], got.at[me], own_sem.at[0]).wait()
+    most = got.at[pl.ds(0, nblk - 1)]
+    pltpu.make_async_copy(most, most, recv_sem.at[0]).wait()
+
+    for i in range(here):
+        x = got[:, i, :]
+        xh, xl = split(jnp.concatenate([x, pltpu.roll(x, chains, 1)], axis=0))
+        y = jnp.dot(gram[i], jnp.concatenate([xh, xl], axis=1), preferred_element_type=F32)
+        wide, two = 2 * chains, 2 * orders
+        y = (y[:two, :wide] + y[:two, wide:]) + (y[two:, :wide] + y[two:, wide:])
+        lane_k = lax.broadcasted_iota(I32, (orders, wide), 1)
+        stage[:, i, :] = jnp.where(lane_k < chains, y[:orders], y[orders:])
+    half[...] = stage[...].astype(BF16)
+
+    for g in range(2):
+
+        def send(d, t, g=g):
+            pltpu.make_async_remote_copy(
+                src_ref=half.at[d], dst_ref=back.at[t], send_sem=send_sem.at[1], recv_sem=recv_sem.at[1 + g],
+                device_id=(band, d), device_id_type=MESH,
+            ).start()
+
+        each_other(send, g * nz // 2, (g + 1) * nz // 2)
+
+    pltpu.make_async_copy(half.at[me], back.at[nblk - 1], own_sem.at[2]).start()
+
     row = lax.broadcasted_iota(I32, (cycles, cycles), 0)
     col = lax.broadcasted_iota(I32, (cycles, cycles), 1)
     slot = col % (nblk // 2) + col // (cycles // 2) * (nblk // 2)
@@ -229,32 +255,6 @@
     pick = jnp.where(row == here * source + col // (nblk // 2) % here, 1.0, 0.0).astype(BF16)
     mine = leg_ref[pl.ds(pl.multiple_of(band * rows, rows & -rows), rows), :]
     legp[...] = jnp.dot(mine, pick, preferred_element_type=F32).astype(BF16)
-
-    pltpu.make_async_copy(syn.at[me], got.at[me], own_sem.at[0]).wait()
-    most = got.at[pl.ds(0, nblk - 1)]
-    pltpu.make_async_copy(most, most, recv_sem.at[0]).wait()
-
-    for i in range(here):
-        x = got[:, i, :]
-        xh, xl = split(jnp.concatenate([x, pltpu.roll(x, chains, 1)], axis=0))
-        y = jnp.dot(gram[i], jnp.concatenate([xh, xl], axis=1), preferred_element_type=F32)
-        wide, two = 2 * chains, 2 * orders
-        y = (y[:two, :wide] + y[:two, wide:]) + (y[two:, :wide] + y[two:, wide:])
-        lane_k = lax.broadcasted_iota(I32, (orders, wide), 1)
-        stage[:, i, :] = jnp.where(lane_k < chains, y[:orders], y[orders:])
-    half[...] = stage[...].astype(BF16)
-
-    for g in range(2):
-
-        def send(d, t, g=g):
-            pltpu.make_async_remote_copy(
-                src_ref=half.at[d], dst_ref=back.at[t], send_sem=send_sem.at[1], recv_sem=recv_sem.at[1 + g],
-                device_id=(band, d), device_id_type=MESH,
-            ).start()
-
-        each_other(send, g * nz // 2, (g + 1) * nz // 2)
-
-    pltpu.make_async_copy(half.at[me], back.at[nblk - 1], own_sem.at[2]).start()
 
     pltpu.make_async_copy(beam_ref, beams.at[band], own_sem.at[1]).wait()
     pltpu.make_async_copy(beams.at[pl.ds(0, nband - 1)], beams.at[pl.ds(0, nband - 1)], beam_sem.at[1]).wait()

time: 43.9 us -> 43.7 us (level)
  no operation moved by 1% of the time
where the time goes in v6:
time: 43.7 us; the launch traced here: 43.6 us
  Pallas kernels  42.9 us (98%)
  other arithmetic  0.69 us (2%)
    pallas_call x1, Pallas kernels, shards(): pl.pallas_call(functools.partial(kernel, nband, nblk), out_shape=[pltpu.V...  42.9 us

profile of v6, /device:TPU:1, one launch (start us, length us, event | category | flops | bytes accessed | tf_op | source)
XLA Modules:
  0.0 43.6 jit_solution(9099784892883785976)
XLA Ops:
  0.0 42.9 %shard_map.73 = (f32[320,128]{1,0:T(8,128)S(1)}, f32[320,128]{1,0:T(8,128)S(1)}) custom-call(s32[64]{0:T(128)} %m_in.1, s32[256]{0:T(256)} %order_in.1, s32[256]{0:T(256)} %counts_in.1, f32[1,2560]{1,0:T(1,128)} %beam_in.1, bf16[2560,128]{1,0:T(8,128)(2,1)} %bitcast.7, bf16[2560,256]{1,0:T(8,128)(2,1)} %bitcast.6, f32[4,4096]{1,0:T(4,128)} %bitcast.8), custom_call_target="tpu_custom_call" | custom-call | tf_op jit(solution)/shard_map/pallas_call | solution.py:349
  42.9 0.7 %add.3 = f32[320,128]{1,0:T(8,128)} add(f32[320,128]{1,0:T(8,128)S(1)} %get-tuple-element.7, f32[320,128]{1,0:T(8,128)S(1)} %get-tuple-element.8) | non-fusion elementwise | flops 40960 | bytes 491520 | tf_op jit(solution)/shard_map/add | solution.py:394
